TPU v7x, 256 devices: a whole 4x4x8 slice. The times are simulated.
256 devices in a mesh: gx: 8 (over x, core), gy: 32 (over z, y).
Axes of the slice: x: 4, y: 4, z: 8, core: 2. Of those that a mesh axis runs over, the one named last changes fastest.
Arguments:
- residual: float32 [1024, 1024, 256], P('gx', 'gy'), may hold values from -6 to 6
- local_x: bfloat16 [136, 136], replicated, may hold values from -0.5 to 0.5
- local_y: bfloat16 [40, 40], replicated, may hold values from -1 to 1
- local_z: bfloat16 [256, 256], replicated, may hold values from -0.375 to 0.375
- eig_x: float32 [136], replicated, may hold values from 0.1 to 2
- eig_y: float32 [40], replicated, may hold values from 0.1 to 2
- eig_z: float32 [256], replicated, may hold values from 0.1 to 2
- coarse_x: bfloat16 [128, 4], replicated, may hold values from -0.5 to 0.5
- coarse_y: bfloat16 [32, 4], replicated, may hold values from -1 to 1
- coarse_z: bfloat16 [256, 4], replicated, may hold values from -0.375 to 0.375
- mode_x: float32 [32, 32], replicated, may hold values from -1 to 1
- mode_y: float32 [128, 128], replicated, may hold values from -0.5 to 0.5
- mode_z: float32 [4, 4], replicated, may hold values from -3 to 3
- coarse_eig_x: float32 [32], replicated, may hold values from 0.002 to 0.02
- coarse_eig_y: float32 [128], replicated, may hold values from 0.002 to 0.02
- coarse_eig_z: float32 [4], replicated, may hold values from 0.002 to 0.02
Outputs:
- preconditioned: float32 [1024, 1024, 256], P('gx', 'gy')
All inputs are finite; a program needn't handle non-finite values.
Results may differ from a plain program's by a relative error of at most 0.0045.
Values may be sent and summed in bfloat16 or wider, within the bound.
No kernel may reach another device: no remote copies, remote signals or barrier semaphores. Data moves between devices by JAX's collectives and lax.ppermute only.
A program may use at most 64 MiB of HBM per device.

v0:
```python
import jax
import jax.numpy as jnp
from jax import lax
from jax.sharding import PartitionSpec as P

OV = 4
MODES = 4


def with_halo(x, sides, width):
    for axis, dim in sides:
        size, length = (lax.axis_size(axis), x.shape[dim])
        up = [(i, (i + 1) % size) for i in range(size)]
        down = [(j, i) for i, j in up]
        last = lax.slice_in_dim(x, length - width, length, axis=dim)
        initial = lax.slice_in_dim(x, 0, width, axis=dim)
        before = lax.ppermute(last, axis, up)
        after = lax.ppermute(initial, axis, down)
        x = jnp.concatenate([before, x, after], axis=dim)
    return x


def solve_local(block, local_x, local_y, local_z, scales):
    first_x = jnp.einsum("xa,xyz->ayz", local_x, block, preferred_element_type=jnp.float32).astype(
        jnp.bfloat16
    )
    first_y = jnp.einsum(
        "yb,ayz->abz", local_y, first_x, preferred_element_type=jnp.float32
    ).astype(jnp.bfloat16)
    along = jnp.einsum("zc,abz->abc", local_z, first_y, preferred_element_type=jnp.float32)
    spectral = (along / scales).astype(jnp.bfloat16)
    back_z = jnp.einsum(
        "zc,abc->abz", local_z, spectral, preferred_element_type=jnp.float32
    ).astype(jnp.bfloat16)
    back_y = jnp.einsum("yb,abz->ayz", local_y, back_z, preferred_element_type=jnp.float32).astype(
        jnp.bfloat16
    )
    return jnp.einsum("xa,ayz->xyz", local_x, back_y, preferred_element_type=jnp.float32)


def strips_rows(field):
    return jnp.concatenate([field[:OV], field[field.shape[0] - OV :]], 0)


def strips_cols(field):
    return jnp.concatenate([field[:, :OV], field[:, field.shape[1] - OV :]], 1)


def add_rows(field, received):
    inner = field[OV : field.shape[0] - OV]
    inner = inner.at[:OV].add(received[:OV])
    return inner.at[inner.shape[0] - OV :].add(received[received.shape[0] - OV :])


def add_cols(field, received):
    inner = field[:, OV : field.shape[1] - OV]
    inner = inner.at[:, :OV].add(received[:, :OV])
    return inner.at[:, inner.shape[1] - OV :].add(received[:, received.shape[1] - OV :])


def local(
    residual,
    local_x,
    local_y,
    local_z,
    eig_x,
    eig_y,
    eig_z,
    coarse_x,
    coarse_y,
    coarse_z,
    mode_x,
    mode_y,
    mode_z,
    coarse_eig_x,
    coarse_eig_y,
    coarse_eig_z,
):
    cells_x, cells_y, levels = residual.shape
    rounded = residual.astype(jnp.bfloat16)
    along_z = jnp.dot(rounded.reshape(-1, levels), coarse_z, preferred_element_type=jnp.float32)
    along_z = along_z.reshape(cells_x, cells_y, MODES)
    basis_x = coarse_x.astype(jnp.float32)
    basis_y = coarse_y.astype(jnp.float32)
    own_coarse = jnp.einsum(
        "xyp,xm,yn->mnp", along_z, basis_x, basis_y, precision=lax.Precision.HIGHEST
    )
    row_index = lax.axis_index("gx")
    col_index = lax.axis_index("gy")
    rows_x = lax.dynamic_slice_in_dim(mode_x, row_index * MODES, MODES, 0)
    rows_y = lax.dynamic_slice_in_dim(mode_y, col_index * MODES, MODES, 0)
    partial_rows = lax.all_gather(own_coarse, "gx", axis=0, tiled=True)
    coarse_res = lax.all_gather(partial_rows, "gy", axis=1, tiled=True)
    coarse_hat = jnp.einsum(
        "IJp,Ia,Jb,pc->abc", coarse_res, mode_x, mode_y, mode_z, precision=lax.Precision.HIGHEST
    )
    coarse_hat = coarse_hat / (
        coarse_eig_x[:, None, None] + coarse_eig_y[None, :, None] + coarse_eig_z[None, None, :]
    )
    own_sol = jnp.einsum(
        "abc,ma,nb,pc->mnp", coarse_hat, rows_x, rows_y, mode_z, precision=lax.Precision.HIGHEST
    )
    spread = jnp.einsum(
        "mnp,xm,yn->xyp", own_sol, basis_x, basis_y, precision=lax.Precision.HIGHEST
    )
    coarse_fix = jnp.dot(
        spread.reshape(-1, MODES), coarse_z.astype(jnp.float32).T, precision=lax.Precision.HIGHEST
    )
    coarse_fix = coarse_fix.reshape(cells_x, cells_y, levels)
    extended = with_halo(rounded, (("gx", 0), ("gy", 1)), OV)
    scales = eig_x[:, None, None] + eig_y[None, :, None] + eig_z[None, None, :]
    local_fix = solve_local(extended, local_x, local_y, local_z, scales)
    received = with_halo(strips_rows(local_fix).astype(jnp.bfloat16), (("gx", 0),), OV).astype(
        jnp.float32
    )
    folded = add_rows(local_fix, received)
    received = with_halo(strips_cols(folded).astype(jnp.bfloat16), (("gy", 1),), OV).astype(
        jnp.float32
    )
    folded = add_cols(folded, received)
    return folded + coarse_fix


def solution(mesh):
    placed = (
        P("gx", "gy", None),
        P(),
        P(),
        P(),
        P(),
        P(),
        P(),
        P(),
        P(),
        P(),
        P(),
        P(),
        P(),
        P(),
        P(),
        P(),
    )
    return jax.shard_map(
        local, mesh=mesh, in_specs=placed, out_specs=P("gx", "gy", None), check_vma=False
    )
```

profile of v0, /device:TPU:1, one launch (start us, length us, event | category | flops | bytes accessed | tf_op | source)
XLA Modules:
  0.0 123.9 jit_solution(12545552153308260391)
XLA Ops:
  0.1 4.5 %copy.79 = bf16[128,32,256]{2,0,1:T(8,128)(2,1)S(1)} copy(f32[128,32,256]{2,1,0:T(8,128)} %param.24) | data formatting | bytes 6291456 | tf_op args[0]
  4.7 2.6 %collective-permute-start = (bf16[4,32,256]{2,0,1:T(4,128)(2,1)S(1)}, bf16[4,32,256]{2,0,1:T(4,128)(2,1)S(1)}, u32[]{:S(2)}, u32[]{:S(2)}) collective-permute-start(bf16[4,32,256]{2,0,1:T(4,128)(2,1)S(1)} %get-tuple-element.59), channel_id=1, source_target_pairs={{0,32},{32,64},{64,96},{96,128},{128,160},{160,192},{192,224},{224... | collective-permute-start | bytes 196616 | tf_op jit(solution)/shard_map/ppermute | solution.py:17
  7.3 0.6 collective-permute-start.1
  7.9 0.6 fusion.61
  8.6 0.2 convolution_bitcast_fusion.4
  9.1 15.5 %all_gather.6 = f32[32,4,4]{2,1,0:T(4,128)S(1)} all-gather(f32[4,4,4]{2,1,0:T(4,128)S(1)} %copy.28), channel_id=1, replica_groups=mesh['gx'=8,'gy'=32] {'gx'}, dimensions={0}, use_global_device_ids=true | all-gather | bytes 2304 | tf_op jit(solution)/shard_map/all_gather | solution.py:92
  24.7 38.5 %all_gather.7 = f32[32,128,4]{0,2,1:T(4,128)S(1)} all-gather(f32[32,4,4]{0,2,1:T(4,128)S(1)} %copy.29), channel_id=1, replica_groups=mesh['gx'=8,'gy'=32] {'gy'}, dimensions={1}, use_global_device_ids=true | all-gather | bytes 67584 | tf_op jit(solution)/shard_map/all_gather | solution.py:93
  63.3 0.4 convolution_bitcast_fusion.1
  63.7 0.2 fusion.41
  64.0 0.3 convolution_divide_fusion
  64.3 0.3 fusion.44
  64.8 0.8 collective-permute-start.2
  65.6 4.0 %collective-permute-start.3 = (bf16[136,4,256]{2,0,1:T(8,128)(2,1)S(1)}, bf16[136,4,256]{2,0,1:T(8,128)(2,1)S(1)}, u32[]{:S(2)}, u32[]{:S(2)}) collective-permute-start(bf16[136,4,256]{2,0,1:T(8,128)(2,1)S(1)} %get-tuple-element.58), channel_id=1, source_target_pairs={{1,0},{2,1},{3,2},{4,3},{5,4},{6,5},{7,6},{8,7},{9,8},{10,9},{11,1... | collective-permute-start | bytes 835592 | tf_op jit(solution)/shard_map/ppermute | solution.py:18
  69.7 0.3 fusion.54
  70.1 3.6 %collective-permute-done.2 = bf16[136,4,256]{2,0,1:T(8,128)(2,1)S(1)} collective-permute-done((bf16[136,4,256]{2,0,1:T(8,128)(2,1)S(1)}, bf16[136,4,256]{2,0,1:T(8,128)(2,1)S(1)}, u32[]{:S(2)}, u32[]{:S(2)}) %collective-permute-start.2) | collective-permute-done | bytes 278560 | tf_op jit(solution)/shard_map/ppermute | solution.py:17
  73.7 2.6 %convert_bitcast_fusion.1 = bf16[136,40,256]{2,0,1:T(8,128)(2,1)} fusion(bf16[136,4,256]{2,0,1:T(8,128)(2,1)S(1)} %collective-permute-done.3, bf16[4,32,256]{2,0,1:T(4,128)(2,1)S(1)} %collective-permute-done.1, bf16[128,32,256]{2,0,1:T(8,128)(2,1)S(1)} %copy.79, bf16[4,32,256]{2,0,1:T(4,128)(2,1)S(1)} %collective-permute-done, ...), kind=kOutput, calls=%fused_computation.22 | convolution fusion | flops 394117120 | bytes 5607552 | tf_op jit(solution)/shard_map/xa,xyz->ayz/dot_general | solution.py:24
  76.3 5.9 %fusion.10 = f32[136,40,256]{2,1,0:T(8,128)} fusion(bf16[136,40,256]{2,0,1:T(8,128)(2,1)} %convert_bitcast_fusion.1, bf16[256,256]{1,0:T(8,128)(2,1)S(1)} %copy-done, bf16[40,40]{1,0:T(8,128)(2,1)S(1)} %copy-done.4), kind=kOutput, calls=%fused_computation.12 | convolution fusion | flops 825835520 | bytes 8490112 | tf_op jit(solution)/shard_map/zc,abz->abc/dot_general | solution.py:30
  82.2 4.6 %convert_bitcast_fusion = bf16[136,40,256]{2,1,0:T(8,128)(2,1)S(1)} fusion(f32[136,40,256]{2,1,0:T(8,128)} %fusion.10, f32[256]{0:T(256)S(1)} %copy-done.13, f32[136,40]{1,0:T(8,128)S(1)} %broadcast_add_fusion, bf16[256,256]{1,0:T(8,128)(2,1)S(1)} %copy-done, bf16[40,40]{1,0:T(8,128)(2,1)S(1)} %copy-done.4), kind=kOutput, calls=%fused_computation.18 | convolution fusion | flops 831406080 | bytes 8512896 | tf_op jit(solution)/shard_map/yb,abz->ayz/dot_general | solution.py:35
  86.9 1.0 fusion.76
  87.9 13.8 %collective-permute-start.4 = (bf16[4,40,256]{2,0,1:T(4,128)(2,1)S(1)}, bf16[4,40,256]{2,0,1:T(4,128)(2,1)S(1)}, u32[]{:S(2)}, u32[]{:S(2)}) collective-permute-start(bf16[4,40,256]{2,0,1:T(4,128)(2,1)S(1)} %get-tuple-element.53), channel_id=1, source_target_pairs={{0,32},{32,64},{64,96},{96,128},{128,160},{160,192},{192,224},{224... | collective-permute-start | bytes 245768 | tf_op jit(solution)/shard_map/ppermute | solution.py:17
  101.9 0.7 slice.168
  102.6 0.5 collective-permute-done.4
  103.1 2.7 %collective-permute-done.5 = bf16[4,40,256]{2,0,1:T(4,128)(2,1)S(1)} collective-permute-done((bf16[4,40,256]{2,0,1:T(4,128)(2,1)S(1)}, bf16[4,40,256]{2,0,1:T(4,128)(2,1)S(1)}, u32[]{:S(2)}, u32[]{:S(2)}) %collective-permute-start.5) | collective-permute-done | bytes 81952 | tf_op jit(solution)/shard_map/ppermute | solution.py:18
  106.0 0.2 fusion.34
  106.2 0.4 convert.13
  106.7 5.4 %collective-permute-start.7 = (bf16[128,4,256]{2,0,1:T(8,128)(2,1)S(1)}, bf16[128,4,256]{2,0,1:T(8,128)(2,1)S(1)}, u32[]{:S(2)}, u32[]{:S(2)}) collective-permute-start(bf16[128,4,256]{2,0,1:T(8,128)(2,1)S(1)} %get-tuple-element.56), channel_id=1, source_target_pairs={{1,0},{2,1},{3,2},{4,3},{5,4},{6,5},{7,6},{8,7},{9,8},{10,9},{11,1... | collective-permute-start | bytes 786440 | tf_op jit(solution)/shard_map/ppermute | solution.py:18
  112.0 0.2 convolution_bitcast_fusion.2
  112.2 0.3 convolution_bitcast_fusion
  112.5 0.3 slice.173
  112.8 4.7 %collective-permute-done.6 = bf16[128,4,256]{2,0,1:T(8,128)(2,1)S(1)} collective-permute-done((bf16[128,4,256]{2,0,1:T(8,128)(2,1)S(1)}, bf16[128,4,256]{2,0,1:T(8,128)(2,1)S(1)}, u32[]{:S(2)}, u32[]{:S(2)}) %collective-permute-start.6) | collective-permute-done | bytes 262176 | tf_op jit(solution)/shard_map/ppermute | solution.py:17
  117.6 1.9 %convolution_add_fusion = f32[128,32,256]{2,0,1:T(8,128)S(1)} fusion(f32[128,32,256]{2,0,1:T(8,128)S(1)} %fusion.31, f32[128,32,4]{0,1,2:T(8,128)S(1)} %convolution_bitcast_fusion, bf16[256,4]{0,1:T(4,128)(2,1)S(1)} %copy-done.5), kind=kOutput, calls=%fused_computation.25 | convolution fusion | flops 51380224 | bytes 8456192 | tf_op jit(solution)/shard_map/dot_general | solution.py:106
  119.5 4.4 %copy.40 = f32[128,32,256]{2,1,0:T(8,128)} copy(f32[128,32,256]{2,0,1:T(8,128)S(1)} %convolution_add_fusion) | data formatting | bytes 8388608 | tf_op jit(solution)/shard_map/add | solution.py:121
  (49 shorter events, 1.6 us)
Async XLA Ops:
  0.0 76.3 %copy-start = (bf16[256,256]{1,0:T(8,128)(2,1)S(1)}, bf16[256,256]{1,0:T(8,128)(2,1)}, u32[]{:S(2)}) copy-start(bf16[256,256]{1,0:T(8,128)(2,1)} %param.27) | copy-start | bytes 393220
  0.0 7.9 %copy-start.5 = (bf16[256,4]{0,1:T(4,128)(2,1)S(1)}, bf16[256,4]{0,1:T(4,128)(2,1)}, u32[]{:S(2)}) copy-start(bf16[256,4]{0,1:T(4,128)(2,1)} %param.33) | copy-start | bytes 6148
  0.0 8.6 %copy-start.6 = (bf16[128,4]{0,1:T(4,128)(2,1)S(1)}, bf16[128,4]{0,1:T(4,128)(2,1)}, u32[]{:S(2)}) copy-start(bf16[128,4]{0,1:T(4,128)(2,1)} %param.31) | copy-start | bytes 3076
  0.0 8.8 %copy-start.7 = (bf16[32,4]{0,1:T(4,128)(2,1)S(1)}, bf16[32,4]{0,1:T(4,128)(2,1)}, u32[]{:S(2)}) copy-start(bf16[32,4]{0,1:T(4,128)(2,1)} %param.32) | copy-start | bytes 772
  0.0 63.2 %copy-start.11 = (f32[128]{0:T(128)S(1)}, f32[128]{0:T(128)}, u32[]{:S(2)}) copy-start(f32[128]{0:T(128)} %param.38) | copy-start | bytes 1540
  0.0 63.2 %copy-start.12 = (f32[32]{0:T(128)S(1)}, f32[32]{0:T(128)}, u32[]{:S(2)}) copy-start(f32[32]{0:T(128)} %param.37) | copy-start | bytes 388
  0.0 63.3 %copy-start.3 = (f32[32,32]{1,0:T(8,128)S(1)}, f32[32,32]{1,0:T(8,128)}, u32[]{:S(2)}) copy-start(f32[32,32]{1,0:T(8,128)} %param.34) | copy-start | bytes 12292
  0.1 63.7 %copy-start.1 = (f32[128,128]{1,0:T(8,128)S(1)}, f32[128,128]{1,0:T(8,128)}, u32[]{:S(2)}) copy-start(f32[128,128]{1,0:T(8,128)} %param.35) | copy-start | bytes 196612
  0.1 63.9 %copy-start.8 = (f32[4,4]{1,0:T(4,128)S(1)}, f32[4,4]{1,0:T(4,128)}, u32[]{:S(2)}) copy-start(f32[4,4]{1,0:T(4,128)} %param.36) | copy-start | bytes 196
  0.1 63.9 %copy-start.14 = (f32[4]{0:T(128)S(1)}, f32[4]{0:T(128)}, u32[]{:S(2)}) copy-start(f32[4]{0:T(128)} %param.39) | copy-start | bytes 52
  4.6 65.4 %copy-start.9 = (f32[136]{0:T(256)S(1)}, f32[136]{0:T(256)}, u32[]{:S(2)}) copy-start(f32[136]{0:T(256)} %param.28) | copy-start | bytes 1636
  4.6 65.4 %copy-start.10 = (f32[40]{0:T(128)S(1)}, f32[40]{0:T(128)}, u32[]{:S(2)}) copy-start(f32[40]{0:T(128)} %param.29) | copy-start | bytes 484
  4.6 69.1 %copy-start.2 = (bf16[136,136]{1,0:T(8,128)(2,1)S(1)}, bf16[136,136]{1,0:T(8,128)(2,1)}, u32[]{:S(2)}) copy-start(bf16[136,136]{1,0:T(8,128)(2,1)} %param.25) | copy-start | bytes 110980
  4.7 59.9 %collective-permute-start = (bf16[4,32,256]{2,0,1:T(4,128)(2,1)S(1)}, bf16[4,32,256]{2,0,1:T(4,128)(2,1)S(1)}, u32[]{:S(2)}, u32[]{:S(2)}) collective-permute-start(bf16[4,32,256]{2,0,1:T(4,128)(2,1)S(1)} %get-tuple-element.59), channel_id=1, source_target_pairs={{0,32},{32,64},{64,96},{96,128},{128,160},{160,192},{192,224},{224... | collective-permute-start | bytes 196616 | tf_op jit(solution)/shard_map/ppermute | solution.py:17
  7.3 57.3 %collective-permute-start.1 = (bf16[4,32,256]{2,0,1:T(4,128)(2,1)S(1)}, bf16[4,32,256]{2,0,1:T(4,128)(2,1)S(1)}, u32[]{:S(2)}, u32[]{:S(2)}) collective-permute-start(bf16[4,32,256]{2,0,1:T(4,128)(2,1)S(1)} %get-tuple-element.60), channel_id=1, source_target_pairs={{32,0},{64,32},{96,64},{128,96},{160,128},{192,160},{224,192},{0,2... | collective-permute-start | bytes 196616 | tf_op jit(solution)/shard_map/ppermute | solution.py:18
  64.8 8.9 %collective-permute-start.2 = (bf16[136,4,256]{2,0,1:T(8,128)(2,1)S(1)}, bf16[136,4,256]{2,0,1:T(8,128)(2,1)S(1)}, u32[]{:S(2)}, u32[]{:S(2)}) collective-permute-start(bf16[136,4,256]{2,0,1:T(8,128)(2,1)S(1)} %get-tuple-element.57), channel_id=1, source_target_pairs={{0,1},{1,2},{2,3},{3,4},{4,5},{5,6},{6,7},{7,8},{8,9},{9,10},{10,1... | collective-permute-start | bytes 835592 | tf_op jit(solution)/shard_map/ppermute | solution.py:17
  65.6 8.1 %collective-permute-start.3 = (bf16[136,4,256]{2,0,1:T(8,128)(2,1)S(1)}, bf16[136,4,256]{2,0,1:T(8,128)(2,1)S(1)}, u32[]{:S(2)}, u32[]{:S(2)}) collective-permute-start(bf16[136,4,256]{2,0,1:T(8,128)(2,1)S(1)} %get-tuple-element.58), channel_id=1, source_target_pairs={{1,0},{2,1},{3,2},{4,3},{5,4},{6,5},{7,6},{8,7},{9,8},{10,9},{11,1... | collective-permute-start | bytes 835592 | tf_op jit(solution)/shard_map/ppermute | solution.py:18
  70.1 6.2 %copy-start.4 = (bf16[40,40]{1,0:T(8,128)(2,1)S(1)}, bf16[40,40]{1,0:T(8,128)(2,1)}, u32[]{:S(2)}) copy-start(bf16[40,40]{1,0:T(8,128)(2,1)} %param.26) | copy-start | bytes 9604
  76.3 5.9 %copy-start.13 = (f32[256]{0:T(256)S(1)}, f32[256]{0:T(256)}, u32[]{:S(2)}) copy-start(f32[256]{0:T(256)} %param.30) | copy-start | bytes 3076
  87.9 15.2 %collective-permute-start.4 = (bf16[4,40,256]{2,0,1:T(4,128)(2,1)S(1)}, bf16[4,40,256]{2,0,1:T(4,128)(2,1)S(1)}, u32[]{:S(2)}, u32[]{:S(2)}) collective-permute-start(bf16[4,40,256]{2,0,1:T(4,128)(2,1)S(1)} %get-tuple-element.53), channel_id=1, source_target_pairs={{0,32},{32,64},{64,96},{96,128},{128,160},{160,192},{192,224},{224... | collective-permute-start | bytes 245768 | tf_op jit(solution)/shard_map/ppermute | solution.py:17
  101.6 4.2 %collective-permute-start.5 = (bf16[4,40,256]{2,0,1:T(4,128)(2,1)S(1)}, bf16[4,40,256]{2,0,1:T(4,128)(2,1)S(1)}, u32[]{:S(2)}, u32[]{:S(2)}) collective-permute-start(bf16[4,40,256]{2,0,1:T(4,128)(2,1)S(1)} %get-tuple-element.54), channel_id=1, source_target_pairs={{32,0},{64,32},{96,64},{128,96},{160,128},{192,160},{224,192},{0,2... | collective-permute-start | bytes 245768 | tf_op jit(solution)/shard_map/ppermute | solution.py:18
  106.6 10.9 %collective-permute-start.6 = (bf16[128,4,256]{2,0,1:T(8,128)(2,1)S(1)}, bf16[128,4,256]{2,0,1:T(8,128)(2,1)S(1)}, u32[]{:S(2)}, u32[]{:S(2)}) collective-permute-start(bf16[128,4,256]{2,0,1:T(8,128)(2,1)S(1)} %get-tuple-element.55), channel_id=1, source_target_pairs={{0,1},{1,2},{2,3},{3,4},{4,5},{5,6},{6,7},{7,8},{8,9},{9,10},{10,1... | collective-permute-start | bytes 786440 | tf_op jit(solution)/shard_map/ppermute | solution.py:17
  106.7 10.8 %collective-permute-start.7 = (bf16[128,4,256]{2,0,1:T(8,128)(2,1)S(1)}, bf16[128,4,256]{2,0,1:T(8,128)(2,1)S(1)}, u32[]{:S(2)}, u32[]{:S(2)}) collective-permute-start(bf16[128,4,256]{2,0,1:T(8,128)(2,1)S(1)} %get-tuple-element.56), channel_id=1, source_target_pairs={{1,0},{2,1},{3,2},{4,3},{5,4},{6,5},{7,6},{8,7},{9,8},{10,9},{11,1... | collective-permute-start | bytes 786440 | tf_op jit(solution)/shard_map/ppermute | solution.py:18
where the time goes:
time: 124 us
  blocking collectives  54 us (44%)
  starting transfers between devices  27.3 us (22%)
  matrix products  19.1 us (15%)
  waiting for transfers between devices  11.5 us (9%)
  local copies, waits for them, and re-layouts  10.4 us (8%)
  other arithmetic  1.26 us (1%)
    all_gather x1, blocking collectives, local(): coarse_res = lax.all_gather(partial_rows, 'gy', axis=1, tiled=True)  38.5 us
    ppermute x4, starting transfers between devices, with_halo(): before = lax.ppermute(last, axis, up)  17.3 us
    all_gather x1, blocking collectives, local(): partial_rows = lax.all_gather(own_coarse, 'gx', axis=0, tiled=True)  15.5 us
    ppermute x4, starting transfers between devices, with_halo(): after = lax.ppermute(initial, axis, down)  10.1 us
    ppermute x4, waiting for transfers between devices, with_halo(): before = lax.ppermute(last, axis, up)  8.78 us
    dot_general x1, matrix products, solve_local(): jnp.einsum('zc,abz->abc', local_z, first_y, preferred_element_type=jnp.fl...  5.94 us
    dot_general x1, matrix products, solve_local(): jnp.einsum('yb,abz->ayz', local_y, back_z, preferred_element_type=jnp.flo...  4.64 us
    unnamed x31, local copies, waits for them, and re-layouts  4.63 us
  transfers between devices with their start and end apart: 8, of which 4 were waited for; matrix products, arithmetic and copies ran while one was open for 4% of the time, Pallas kernels for 0%

commit v1 on v0

--- a/solution.py
+++ b/solution.py
@@ -89,7 +89,9 @@
     col_index = lax.axis_index("gy")
     rows_x = lax.dynamic_slice_in_dim(mode_x, row_index * MODES, MODES, 0)
     rows_y = lax.dynamic_slice_in_dim(mode_y, col_index * MODES, MODES, 0)
-    partial_rows = lax.all_gather(own_coarse, "gx", axis=0, tiled=True)
+    partial_rows = jnp.concatenate(
+        lax.all_to_all(jnp.stack([own_coarse] * lax.axis_size("gx")), "gx", 0, 0), axis=0
+    )
     coarse_res = lax.all_gather(partial_rows, "gy", axis=1, tiled=True)
     coarse_hat = jnp.einsum(
         "IJp,Ia,Jb,pc->abc", coarse_res, mode_x, mode_y, mode_z, precision=lax.Precision.HIGHEST

time: 124 us -> 119 us (0.960)
  blocking collectives: 54 us -> 39.8 us
  starting transfers between devices: 27.3 us -> 33 us
  waiting for transfers between devices: 11.5 us -> 14.5 us
    all_gather x1 -> x0, blocking collectives: 15.5 us -> none  [local(): partial_rows = lax.all_gather(own_coarse, 'gx', axis=0, tiled=True)]
    all_to_all x0 -> x1, starting transfers between devices: none -> 6.44 us  [local(): lax.all_to_all(jnp.stack([own_coarse] * lax.axis_size('gx')), 'gx', 0, 0)]
    all_to_all x0 -> x1, waiting for transfers between devices: none -> 2.97 us  [local(): lax.all_to_all(jnp.stack([own_coarse] * lax.axis_size('gx')), 'gx', 0, 0)]
    all_gather x1, blocking collectives: 38.5 us -> 39.8 us  [local(): coarse_res = lax.all_gather(partial_rows, 'gy', axis=1, tiled=True)]
  transfers between devices with their start and end apart: 8 -> 9, of which waited for: 4 -> 5; matrix products, arithmetic and copies ran while one was open for 4% -> 3% of each run, Pallas kernels for 0% -> 0%
where the time goes in v1:
time: 119 us
  blocking collectives  39.8 us (33%)
  starting transfers between devices  33 us (28%)
  matrix products  19.2 us (16%)
  waiting for transfers between devices  14.5 us (12%)
  local copies, waits for them, and re-layouts  11.1 us (9%)
  other arithmetic  1.2 us (1%)
    all_gather x1, blocking collectives, local(): coarse_res = lax.all_gather(partial_rows, 'gy', axis=1, tiled=True)  39.8 us
    ppermute x4, starting transfers between devices, with_halo(): before = lax.ppermute(last, axis, up)  17 us
    ppermute x4, starting transfers between devices, with_halo(): after = lax.ppermute(initial, axis, down)  9.55 us
    ppermute x4, waiting for transfers between devices, with_halo(): before = lax.ppermute(last, axis, up)  8.81 us
    all_to_all x1, starting transfers between devices, local(): lax.all_to_all(jnp.stack([own_coarse] * lax.axis_size('gx')), 'gx', 0, 0)  6.44 us
    dot_general x1, matrix products, solve_local(): jnp.einsum('zc,abz->abc', local_z, first_y, preferred_element_type=jnp.fl...  5.95 us
    dot_general x1, matrix products, solve_local(): jnp.einsum('yb,abz->ayz', local_y, back_z, preferred_element_type=jnp.flo...  4.64 us
    unnamed x31, local copies, waits for them, and re-layouts  4.61 us
  transfers between devices with their start and end apart: 9, of which 5 were waited for; matrix products, arithmetic and copies ran while one was open for 3% of the time, Pallas kernels for 0%

profile of v1, /device:TPU:1, one launch (start us, length us, event | category | flops | bytes accessed | tf_op | source)
XLA Modules:
  0.0 119.0 jit_solution(1453546534950071791)
XLA Ops:
  0.1 4.5 %copy.99 = bf16[128,32,256]{2,0,1:T(8,128)(2,1)S(1)} copy(f32[128,32,256]{2,1,0:T(8,128)} %param.24) | data formatting | bytes 6291456 | tf_op args[0]
  4.6 0.6 fusion.61
  5.3 0.2 convolution_bitcast_fusion.4
  5.8 0.6 stack.2
  6.5 6.4 %all-to-all-start = ((f32[8,4,4,4]{1,3,2,0:T(4,128)}), f32[8,4,4,4]{1,3,2,0:T(4,128)S(1)}, u32[]{:S(2)}, u32[]{:S(2)}) async-start(f32[8,4,4,4]{1,3,2,0:T(4,128)} %stack.2), calls=%async_computation | async-start | bytes 131072 | tf_op jit(solution)/shard_map/all_to_all | solution.py:93
  13.0 1.6 %collective-permute-start = (bf16[4,32,256]{2,0,1:T(4,128)(2,1)S(1)}, bf16[4,32,256]{2,0,1:T(4,128)(2,1)S(1)}, u32[]{:S(2)}, u32[]{:S(2)}) collective-permute-start(bf16[4,32,256]{2,0,1:T(4,128)(2,1)S(1)} %get-tuple-element.59), channel_id=1, source_target_pairs={{0,32},{32,64},{64,96},{96,128},{128,160},{160,192},{192,224},{224... | collective-permute-start | bytes 196616 | tf_op jit(solution)/shard_map/ppermute | solution.py:17
  14.8 3.0 %all-to-all-done = f32[8,4,4,4]{1,3,2,0:T(4,128)S(1)} async-done(((f32[8,4,4,4]{1,3,2,0:T(4,128)}), f32[8,4,4,4]{1,3,2,0:T(4,128)S(1)}, u32[]{:S(2)}, u32[]{:S(2)}) %all-to-all-start) | async-done | bytes 2080 | tf_op jit(solution)/shard_map/all_to_all | solution.py:93
  17.9 39.8 %all_gather.3 = f32[32,128,4]{0,2,1:T(4,128)S(1)} all-gather(f32[32,4,4]{0,2,1:T(4,128)S(1)} %reshape.196), channel_id=1, replica_groups=mesh['gx'=8,'gy'=32] {'gy'}, dimensions={1}, use_global_device_ids=true | all-gather | bytes 67584 | tf_op jit(solution)/shard_map/all_gather | solution.py:95
  57.7 0.4 convolution_bitcast_fusion.1
  58.1 0.2 fusion.41
  58.3 0.3 convolution_divide_fusion
  58.8 0.7 collective-permute-start.2
  59.5 4.2 %collective-permute-start.3 = (bf16[136,4,256]{2,0,1:T(8,128)(2,1)S(1)}, bf16[136,4,256]{2,0,1:T(8,128)(2,1)S(1)}, u32[]{:S(2)}, u32[]{:S(2)}) collective-permute-start(bf16[136,4,256]{2,0,1:T(8,128)(2,1)S(1)} %get-tuple-element.58), channel_id=1, source_target_pairs={{1,0},{2,1},{3,2},{4,3},{5,4},{6,5},{7,6},{8,7},{9,8},{10,9},{11,1... | collective-permute-start | bytes 835592 | tf_op jit(solution)/shard_map/ppermute | solution.py:18
  63.7 0.3 fusion.44
  64.0 0.3 fusion.54
  64.4 3.3 %collective-permute-done.2 = bf16[136,4,256]{2,0,1:T(8,128)(2,1)S(1)} collective-permute-done((bf16[136,4,256]{2,0,1:T(8,128)(2,1)S(1)}, bf16[136,4,256]{2,0,1:T(8,128)(2,1)S(1)}, u32[]{:S(2)}, u32[]{:S(2)}) %collective-permute-start.2) | collective-permute-done | bytes 278560 | tf_op jit(solution)/shard_map/ppermute | solution.py:17
  67.7 2.6 %convert_bitcast_fusion.1 = bf16[136,40,256]{2,0,1:T(8,128)(2,1)} fusion(bf16[136,4,256]{2,0,1:T(8,128)(2,1)S(1)} %collective-permute-done.3, bf16[4,32,256]{2,0,1:T(4,128)(2,1)S(1)} %collective-permute-done.1, bf16[128,32,256]{2,0,1:T(8,128)(2,1)S(1)} %copy.99, bf16[4,32,256]{2,0,1:T(4,128)(2,1)S(1)} %collective-permute-done, ...), kind=kOutput, calls=%fused_computation.22 | convolution fusion | flops 394117120 | bytes 5607552 | tf_op jit(solution)/shard_map/xa,xyz->ayz/dot_general | solution.py:24
  70.3 6.0 %fusion.10 = f32[136,40,256]{2,1,0:T(8,128)} fusion(bf16[136,40,256]{2,0,1:T(8,128)(2,1)} %convert_bitcast_fusion.1, bf16[256,256]{1,0:T(8,128)(2,1)S(1)} %copy-done, bf16[40,40]{1,0:T(8,128)(2,1)S(1)} %copy-done.4), kind=kOutput, calls=%fused_computation.12 | convolution fusion | flops 825835520 | bytes 8490112 | tf_op jit(solution)/shard_map/zc,abz->abc/dot_general | solution.py:30
  76.3 4.6 %convert_bitcast_fusion = bf16[136,40,256]{2,1,0:T(8,128)(2,1)S(1)} fusion(f32[136,40,256]{2,1,0:T(8,128)} %fusion.10, f32[256]{0:T(256)S(1)} %copy-done.13, f32[136,40]{1,0:T(8,128)S(1)} %broadcast_add_fusion, bf16[256,256]{1,0:T(8,128)(2,1)S(1)} %copy-done, bf16[40,40]{1,0:T(8,128)(2,1)S(1)} %copy-done.4), kind=kOutput, calls=%fused_computation.18 | convolution fusion | flops 831406080 | bytes 8512896 | tf_op jit(solution)/shard_map/yb,abz->ayz/dot_general | solution.py:35
  80.9 1.0 fusion.76
  81.9 14.6 %collective-permute-start.4 = (bf16[4,40,256]{2,0,1:T(4,128)(2,1)S(1)}, bf16[4,40,256]{2,0,1:T(4,128)(2,1)S(1)}, u32[]{:S(2)}, u32[]{:S(2)}) collective-permute-start(bf16[4,40,256]{2,0,1:T(4,128)(2,1)S(1)} %get-tuple-element.53), channel_id=1, source_target_pairs={{0,32},{32,64},{64,96},{96,128},{128,160},{160,192},{192,224},{224... | collective-permute-start | bytes 245768 | tf_op jit(solution)/shard_map/ppermute | solution.py:17
  96.7 0.7 slice.168
  97.4 0.6 collective-permute-done.4
  98.0 2.7 %collective-permute-done.5 = bf16[4,40,256]{2,0,1:T(4,128)(2,1)S(1)} collective-permute-done((bf16[4,40,256]{2,0,1:T(4,128)(2,1)S(1)}, bf16[4,40,256]{2,0,1:T(4,128)(2,1)S(1)}, u32[]{:S(2)}, u32[]{:S(2)}) %collective-permute-start.5) | collective-permute-done | bytes 81952 | tf_op jit(solution)/shard_map/ppermute | solution.py:18
  100.8 0.2 fusion.34
  101.1 0.4 convert.13
  101.5 5.4 %collective-permute-start.7 = (bf16[128,4,256]{2,0,1:T(8,128)(2,1)S(1)}, bf16[128,4,256]{2,0,1:T(8,128)(2,1)S(1)}, u32[]{:S(2)}, u32[]{:S(2)}) collective-permute-start(bf16[128,4,256]{2,0,1:T(8,128)(2,1)S(1)} %get-tuple-element.56), channel_id=1, source_target_pairs={{1,0},{2,1},{3,2},{4,3},{5,4},{6,5},{7,6},{8,7},{9,8},{10,9},{11,1... | collective-permute-start | bytes 786440 | tf_op jit(solution)/shard_map/ppermute | solution.py:18
  107.1 0.3 convolution_bitcast_fusion
  107.4 0.3 slice.173
  107.6 4.9 %collective-permute-done.6 = bf16[128,4,256]{2,0,1:T(8,128)(2,1)S(1)} collective-permute-done((bf16[128,4,256]{2,0,1:T(8,128)(2,1)S(1)}, bf16[128,4,256]{2,0,1:T(8,128)(2,1)S(1)}, u32[]{:S(2)}, u32[]{:S(2)}) %collective-permute-start.6) | collective-permute-done | bytes 262176 | tf_op jit(solution)/shard_map/ppermute | solution.py:17
  112.7 1.9 %convolution_add_fusion = f32[128,32,256]{2,0,1:T(8,128)S(1)} fusion(f32[128,32,256]{2,0,1:T(8,128)S(1)} %fusion.31, f32[128,32,4]{0,1,2:T(8,128)S(1)} %convolution_bitcast_fusion, bf16[256,4]{0,1:T(4,128)(2,1)S(1)} %copy-done.5), kind=kOutput, calls=%fused_computation.25 | convolution fusion | flops 51380224 | bytes 8456192 | tf_op jit(solution)/shard_map/dot_general | solution.py:108
  114.6 4.4 %copy.60 = f32[128,32,256]{2,1,0:T(8,128)} copy(f32[128,32,256]{2,0,1:T(8,128)S(1)} %convolution_add_fusion) | data formatting | bytes 8388608 | tf_op jit(solution)/shard_map/add | solution.py:123
  (52 shorter events, 1.7 us)
Async XLA Ops:
  0.0 70.3 %copy-start = (bf16[256,256]{1,0:T(8,128)(2,1)S(1)}, bf16[256,256]{1,0:T(8,128)(2,1)}, u32[]{:S(2)}) copy-start(bf16[256,256]{1,0:T(8,128)(2,1)} %param.27) | copy-start | bytes 393220
  0.0 4.6 %copy-start.5 = (bf16[256,4]{0,1:T(4,128)(2,1)S(1)}, bf16[256,4]{0,1:T(4,128)(2,1)}, u32[]{:S(2)}) copy-start(bf16[256,4]{0,1:T(4,128)(2,1)} %param.33) | copy-start | bytes 6148
  0.0 5.3 %copy-start.6 = (bf16[128,4]{0,1:T(4,128)(2,1)S(1)}, bf16[128,4]{0,1:T(4,128)(2,1)}, u32[]{:S(2)}) copy-start(bf16[128,4]{0,1:T(4,128)(2,1)} %param.31) | copy-start | bytes 3076
  0.0 5.5 %copy-start.7 = (bf16[32,4]{0,1:T(4,128)(2,1)S(1)}, bf16[32,4]{0,1:T(4,128)(2,1)}, u32[]{:S(2)}) copy-start(bf16[32,4]{0,1:T(4,128)(2,1)} %param.32) | copy-start | bytes 772
  0.0 14.6 %copy-start.10 = (f32[40]{0:T(128)S(1)}, f32[40]{0:T(128)}, u32[]{:S(2)}) copy-start(f32[40]{0:T(128)} %param.29) | copy-start | bytes 484
  0.0 14.6 %copy-start.9 = (f32[136]{0:T(256)S(1)}, f32[136]{0:T(256)}, u32[]{:S(2)}) copy-start(f32[136]{0:T(256)} %param.28) | copy-start | bytes 1636
  0.0 14.7 %copy-start.11 = (f32[128]{0:T(128)S(1)}, f32[128]{0:T(128)}, u32[]{:S(2)}) copy-start(f32[128]{0:T(128)} %param.38) | copy-start | bytes 1540
  0.1 14.7 %copy-start.12 = (f32[32]{0:T(128)S(1)}, f32[32]{0:T(128)}, u32[]{:S(2)}) copy-start(f32[32]{0:T(128)} %param.37) | copy-start | bytes 388
  0.1 57.6 %copy-start.3 = (f32[32,32]{1,0:T(8,128)S(1)}, f32[32,32]{1,0:T(8,128)}, u32[]{:S(2)}) copy-start(f32[32,32]{1,0:T(8,128)} %param.34) | copy-start | bytes 12292
  0.1 58.0 %copy-start.1 = (f32[128,128]{1,0:T(8,128)S(1)}, f32[128,128]{1,0:T(8,128)}, u32[]{:S(2)}) copy-start(f32[128,128]{1,0:T(8,128)} %param.35) | copy-start | bytes 196612
  0.1 58.2 %copy-start.8 = (f32[4,4]{1,0:T(4,128)S(1)}, f32[4,4]{1,0:T(4,128)}, u32[]{:S(2)}) copy-start(f32[4,4]{1,0:T(4,128)} %param.36) | copy-start | bytes 196
  0.1 58.2 %copy-start.14 = (f32[4]{0:T(128)S(1)}, f32[4]{0:T(128)}, u32[]{:S(2)}) copy-start(f32[4]{0:T(128)} %param.39) | copy-start | bytes 52
  4.6 63.1 %copy-start.2 = (bf16[136,136]{1,0:T(8,128)(2,1)S(1)}, bf16[136,136]{1,0:T(8,128)(2,1)}, u32[]{:S(2)}) copy-start(bf16[136,136]{1,0:T(8,128)(2,1)} %param.25) | copy-start | bytes 110980
  6.5 11.3 %all-to-all-start = ((f32[8,4,4,4]{1,3,2,0:T(4,128)}), f32[8,4,4,4]{1,3,2,0:T(4,128)S(1)}, u32[]{:S(2)}, u32[]{:S(2)}) async-start(f32[8,4,4,4]{1,3,2,0:T(4,128)} %stack.2), calls=%async_computation | async-start | bytes 131072 | tf_op jit(solution)/shard_map/all_to_all | solution.py:93
  13.0 45.7 %collective-permute-start = (bf16[4,32,256]{2,0,1:T(4,128)(2,1)S(1)}, bf16[4,32,256]{2,0,1:T(4,128)(2,1)S(1)}, u32[]{:S(2)}, u32[]{:S(2)}) collective-permute-start(bf16[4,32,256]{2,0,1:T(4,128)(2,1)S(1)} %get-tuple-element.59), channel_id=1, source_target_pairs={{0,32},{32,64},{64,96},{96,128},{128,160},{160,192},{192,224},{224... | collective-permute-start | bytes 196616 | tf_op jit(solution)/shard_map/ppermute | solution.py:17
  14.6 44.1 %collective-permute-start.1 = (bf16[4,32,256]{2,0,1:T(4,128)(2,1)S(1)}, bf16[4,32,256]{2,0,1:T(4,128)(2,1)S(1)}, u32[]{:S(2)}, u32[]{:S(2)}) collective-permute-start(bf16[4,32,256]{2,0,1:T(4,128)(2,1)S(1)} %get-tuple-element.60), channel_id=1, source_target_pairs={{32,0},{64,32},{96,64},{128,96},{160,128},{192,160},{224,192},{0,2... | collective-permute-start | bytes 196616 | tf_op jit(solution)/shard_map/ppermute | solution.py:18
  58.8 8.9 %collective-permute-start.2 = (bf16[136,4,256]{2,0,1:T(8,128)(2,1)S(1)}, bf16[136,4,256]{2,0,1:T(8,128)(2,1)S(1)}, u32[]{:S(2)}, u32[]{:S(2)}) collective-permute-start(bf16[136,4,256]{2,0,1:T(8,128)(2,1)S(1)} %get-tuple-element.57), channel_id=1, source_target_pairs={{0,1},{1,2},{2,3},{3,4},{4,5},{5,6},{6,7},{7,8},{8,9},{9,10},{10,1... | collective-permute-start | bytes 835592 | tf_op jit(solution)/shard_map/ppermute | solution.py:17
  59.5 8.2 %collective-permute-start.3 = (bf16[136,4,256]{2,0,1:T(8,128)(2,1)S(1)}, bf16[136,4,256]{2,0,1:T(8,128)(2,1)S(1)}, u32[]{:S(2)}, u32[]{:S(2)}) collective-permute-start(bf16[136,4,256]{2,0,1:T(8,128)(2,1)S(1)} %get-tuple-element.58), channel_id=1, source_target_pairs={{1,0},{2,1},{3,2},{4,3},{5,4},{6,5},{7,6},{8,7},{9,8},{10,9},{11,1... | collective-permute-start | bytes 835592 | tf_op jit(solution)/shard_map/ppermute | solution.py:18
  64.4 5.9 %copy-start.4 = (bf16[40,40]{1,0:T(8,128)(2,1)S(1)}, bf16[40,40]{1,0:T(8,128)(2,1)}, u32[]{:S(2)}) copy-start(bf16[40,40]{1,0:T(8,128)(2,1)} %param.26) | copy-start | bytes 9604
  70.3 6.0 %copy-start.13 = (f32[256]{0:T(256)S(1)}, f32[256]{0:T(256)}, u32[]{:S(2)}) copy-start(f32[256]{0:T(256)} %param.30) | copy-start | bytes 3076
  81.9 16.1 %collective-permute-start.4 = (bf16[4,40,256]{2,0,1:T(4,128)(2,1)S(1)}, bf16[4,40,256]{2,0,1:T(4,128)(2,1)S(1)}, u32[]{:S(2)}, u32[]{:S(2)}) collective-permute-start(bf16[4,40,256]{2,0,1:T(4,128)(2,1)S(1)} %get-tuple-element.53), channel_id=1, source_target_pairs={{0,32},{32,64},{64,96},{96,128},{128,160},{160,192},{192,224},{224... | collective-permute-start | bytes 245768 | tf_op jit(solution)/shard_map/ppermute | solution.py:17
  96.5 4.2 %collective-permute-start.5 = (bf16[4,40,256]{2,0,1:T(4,128)(2,1)S(1)}, bf16[4,40,256]{2,0,1:T(4,128)(2,1)S(1)}, u32[]{:S(2)}, u32[]{:S(2)}) collective-permute-start(bf16[4,40,256]{2,0,1:T(4,128)(2,1)S(1)} %get-tuple-element.54), channel_id=1, source_target_pairs={{32,0},{64,32},{96,64},{128,96},{160,128},{192,160},{224,192},{0,2... | collective-permute-start | bytes 245768 | tf_op jit(solution)/shard_map/ppermute | solution.py:18
  101.5 11.1 %collective-permute-start.6 = (bf16[128,4,256]{2,0,1:T(8,128)(2,1)S(1)}, bf16[128,4,256]{2,0,1:T(8,128)(2,1)S(1)}, u32[]{:S(2)}, u32[]{:S(2)}) collective-permute-start(bf16[128,4,256]{2,0,1:T(8,128)(2,1)S(1)} %get-tuple-element.55), channel_id=1, source_target_pairs={{0,1},{1,2},{2,3},{3,4},{4,5},{5,6},{6,7},{7,8},{8,9},{9,10},{10,1... | collective-permute-start | bytes 786440 | tf_op jit(solution)/shard_map/ppermute | solution.py:17
  101.5 11.0 %collective-permute-start.7 = (bf16[128,4,256]{2,0,1:T(8,128)(2,1)S(1)}, bf16[128,4,256]{2,0,1:T(8,128)(2,1)S(1)}, u32[]{:S(2)}, u32[]{:S(2)}) collective-permute-start(bf16[128,4,256]{2,0,1:T(8,128)(2,1)S(1)} %get-tuple-element.56), channel_id=1, source_target_pairs={{1,0},{2,1},{3,2},{4,3},{5,4},{6,5},{7,6},{8,7},{9,8},{10,9},{11,1... | collective-permute-start | bytes 786440 | tf_op jit(solution)/shard_map/ppermute | solution.py:18
